TPU v7x, 32 devices: a whole 2x2x4 slice. The times are simulated.
32 devices in a mesh: row: 4 (over x, core), col: 8 (over z, y).
Axes of the slice: x: 2, y: 2, z: 4, core: 2. Of those that a mesh axis runs over, the one named last changes fastest.
Arguments:
- features: bfloat16 [8192, 256], P(('col', 'row')), may hold values from -6 to 6
- weight: bfloat16 [256, 256], replicated, may hold values from -0.375 to 0.375
- grad_out: bfloat16 [8192, 256], P(('row', 'col')), may hold values from -6 to 6
- adj_values: bfloat16 [384, 1024, 128], P('row', 'col'), may hold values from -0.15625 to 0.15625
- block_pos: int32 [4, 768], P('row', 'col'), may hold values from 0 to 127, as said below
- block_count: int32 [4, 8], P('row', 'col'), may hold values from 24 to 96, as said below
Outputs:
- activation: bfloat16 [8192, 256], P(('row', 'col'))
- grad_input: bfloat16 [8192, 256], P(('col', 'row'))
- grad_weight: float32 [256, 256], replicated
Inputs may be any that keep to these rules, and one draw needn't show every extreme that they name: `block_pos`: within one tile the block positions of all 96 slots are distinct values below 128. `block_count`: some tile has exactly 96 live slots and some tile exactly 24.
All inputs are finite; a program needn't handle non-finite values.
Results may differ from a plain program's by a relative error of at most 0.018.
Values may be sent and summed in bfloat16 or wider, within the bound.
A program may use at most 128 MiB of HBM per device.

v0:
```python
import functools

import jax
import jax.numpy as jnp
from jax import lax
from jax.experimental import pallas as pl
from jax.experimental.pallas import tpu as pltpu
from jax.sharding import PartitionSpec as P

MESH = pl.DeviceIdType.MESH
F32 = jnp.float32
BF16 = jnp.bfloat16


def split_axis(size, inner):
    while size % inner:
        inner -= 1
    return size // inner, inner


class Reduce:
    def __init__(self, link, axis, outer, inner, n_out, n_in, part, bufs, sems):
        self.link, self.axis, self.part = link, axis, part
        self.outer, self.inner, self.n_out, self.n_in = outer, inner, n_out, n_in
        self.s_in, self.r_in, self.s_out, self.r_out = bufs
        self.sem_in, self.sem_out = sems
        self.sent, self.totals, self.held, self.line = [], {}, {}, None

    def to(self, d):
        return lax.rem(self.outer + d, self.n_out)

    def start(self, h, d):
        to = self.to(d)
        for e in range(1, self.n_in):
            peer = lax.rem(self.inner + e, self.n_in)
            slot = (h * self.n_out + d) * (self.n_in - 1) + e - 1
            there = (h * self.n_out + to) * (self.n_in - 1) + e - 1
            self.s_in[slot] = self.part(to * self.n_in + peer, h).astype(BF16)
            copy = self.link(
                self.s_in.at[slot],
                self.r_in.at[there],
                self.sem_in.at[0, slot],
                self.sem_in.at[1, there],
                self.axis,
                self.outer * self.n_in + peer,
            )
            copy.start()
            self.sent.append(copy)

    def middle(self, h, d):
        to = self.to(d)
        value = self.part(to * self.n_in + self.inner, h)
        for e in range(1, self.n_in):
            at = (h * self.n_out + to) * (self.n_in - 1) + e - 1
            self.link(
                self.r_in.at[at],
                self.r_in.at[at],
                self.sem_in.at[0, 0],
                self.sem_in.at[1, at],
                self.axis,
                0,
            ).wait_recv()
            value = value + self.r_in[at].astype(F32)
        if d == 0:
            self.totals[h] = value
            return
        slot = h * (self.n_out - 1) + d - 1
        self.s_out[slot] = value.astype(BF16)
        copy = self.link(
            self.s_out.at[slot],
            self.r_out.at[slot],
            self.sem_out.at[0, slot],
            self.sem_out.at[1, slot],
            self.axis,
            to * self.n_in + self.inner,
        )
        copy.start()
        self.sent.append(copy)

    def end(self, h):
        total = self.totals[h]
        for d in range(1, self.n_out):
            slot = h * (self.n_out - 1) + d - 1
            self.link(
                self.r_out.at[slot],
                self.r_out.at[slot],
                self.sem_out.at[0, slot],
                self.sem_out.at[1, slot],
                self.axis,
                0,
            ).wait_recv()
            total = total + self.r_out[slot].astype(F32)
        return total


class Gather:
    def __init__(self, link, axis, outer, inner, n_out, n_in, halves, buf, send, recv):
        self.link, self.axis, self.halves = link, axis, halves
        self.outer, self.inner, self.n_out, self.n_in = outer, inner, n_out, n_in
        self.buf, self.send, self.recv = buf, send, recv
        self.me = outer * n_in + inner
        self.sent, self.maybe, self.slots, self.line = [], [], 0, None

    def push(self, block, h, peer):
        at = block * self.halves + h
        copy = self.link(
            self.buf.at[at],
            self.buf.at[at],
            self.send.at[len(self.sent) + self.slots],
            self.recv.at[at],
            self.axis,
            peer,
        )
        copy.start()
        self.sent.append(copy)

    def arrive(self, block, h):
        at = block * self.halves + h
        self.link(
            self.buf.at[at], self.buf.at[at], self.send.at[0], self.recv.at[at], self.axis, 0
        ).wait_recv()

    def forward(self, block, h):
        for e in range(1, self.n_in):
            self.push(block, h, self.outer * self.n_in + lax.rem(self.inner + e, self.n_in))

    def start(self, h):
        for d in range(self.n_out - 1, 0, -1):
            self.push(self.me, h, lax.rem(self.outer + d, self.n_out) * self.n_in + self.inner)
        self.forward(self.me, h)

    def from_outer(self, h, d):
        block = lax.rem(self.outer + d, self.n_out) * self.n_in + self.inner
        self.arrive(block, h)
        self.forward(block, h)
        return [block]

    def from_inner(self, h, d):
        blocks = []
        for e in range(1, self.n_in):
            block = lax.rem(self.outer + d, self.n_out) * self.n_in + lax.rem(
                self.inner + e, self.n_in
            )
            self.arrive(block, h)
            blocks.append(block)
        return blocks


class Line:
    def __init__(self, at):
        self.central = lax.rem(lax.div(at + 1, 2), 2) == 1
        self.mate = at + 1 - 2 * lax.rem(at, 2)
        self.near = 2 - lax.div(at, 2)
        self.place = (at, self.mate, self.near, 3 * (self.near - 1))


class TreeReduce(Reduce):
    def to(self, d):
        return self.line.place[d]

    def hop(self, h, d, peer, landing):
        slot = h * 4 + d
        copy = self.link(
            self.s_out.at[slot],
            self.r_out.at[h * 4 + landing],
            self.sem_out.at[0, slot],
            self.sem_out.at[1, h * 4 + landing],
            self.axis,
            peer * self.n_in + self.inner,
        )
        copy.start()
        self.sent.append(copy)

    def landed(self, h, slot):
        at = h * 4 + slot
        self.link(
            self.r_out.at[at],
            self.r_out.at[at],
            self.sem_out.at[0, at],
            self.sem_out.at[1, at],
            self.axis,
            0,
        ).wait_recv()
        return self.r_out[at].astype(F32)

    def middle(self, h, d):
        value = self.part(self.to(d) * self.n_in + self.inner, h)
        for e in range(1, self.n_in):
            at = (h * self.n_out + self.to(d)) * (self.n_in - 1) + e - 1
            self.link(
                self.r_in.at[at],
                self.r_in.at[at],
                self.sem_in.at[0, 0],
                self.sem_in.at[1, at],
                self.axis,
                0,
            ).wait_recv()
            value = value + self.r_in[at].astype(F32)
        line = self.line
        if d == 0:
            self.totals[h] = value
        elif d == 1:
            self.s_out[h * 4 + d] = value.astype(BF16)
            self.hop(h, d, line.mate, 0)
        else:
            self.s_out[h * 4 + d] = value.astype(BF16)
            rim = jnp.logical_not(line.central)

            @pl.when(rim)
            def _():
                self.hop(h, d, line.mate, d)

            self.sent.pop()
            self.held[h, d] = value

    def join(self, h, d):
        line = self.line

        @pl.when(line.central)
        def _():
            total = self.held[h, d] + self.landed(h, d)
            self.s_out[h * 4 + d] = total.astype(BF16)
            self.hop(h, d, line.place[d], 1)

        self.sent.pop()
        slot = h * 4 + d
        self.sent.append(
            self.link(
                self.s_out.at[slot],
                self.s_out.at[slot],
                self.sem_out.at[0, slot],
                self.sem_out.at[1, slot],
                self.axis,
                0,
            )
        )

    def end(self, h):
        return self.totals[h] + self.landed(h, 0) + self.landed(h, 1)


class TreeGather(Gather):
    def start(self, h):
        self.push(self.me, h, self.line.near * self.n_in + self.inner)
        self.push(self.me, h, self.line.mate * self.n_in + self.inner)
        self.forward(self.me, h)

    def from_outer(self, h, d):
        block = self.line.place[d] * self.n_in + self.inner
        self.arrive(block, h)
        if d > 1:

            @pl.when(self.line.central)
            def _():
                self.push(block, h, self.line.mate * self.n_in + self.inner)

            self.sent.pop()
            at = self.me * self.halves + h
            self.maybe.append(
                self.link(
                    self.buf.at[at],
                    self.buf.at[at],
                    self.send.at[len(self.sent) + self.slots],
                    self.recv.at[at],
                    self.axis,
                    0,
                )
            )
            self.slots += 1
        self.forward(block, h)
        return [block]

    def from_inner(self, h, d):
        blocks = []
        for e in range(1, self.n_in):
            block = self.line.place[d] * self.n_in + lax.rem(self.inner + e, self.n_in)
            self.arrive(block, h)
            blocks.append(block)
        return blocks


def kernel(
    dims,
    count_ref,
    pos_ref,
    feat_ref,
    weight_ref,
    gout_ref,
    adj_ref,
    act_ref,
    gin_ref,
    gw_ref,
    inv_v,
    inv_s,
    vals,
    dense,
    dense_t,
    feats,
    wbuf,
    gout,
    cs_y,
    cr_y,
    cs_z,
    cr_z,
    af,
    ghs,
    acc,
    rs_y,
    rr_y,
    rs_z,
    rr_z,
    ws1,
    wr1,
    ws2,
    wr2,
    w4,
    local_sem,
    sem_f,
    sem_fr,
    sem_cy,
    sem_cz,
    sem_g,
    sem_gr,
    sem_ry,
    sem_rz,
    sem_w1,
    sem_w2,
    sem_w3,
    sem_w3r,
    sem_w4,
    sem_w4r,
):
    (nrow, ncol, ro, ri, co, ci, halves) = dims
    slots, bs, _ = adj_ref.shape
    own, width = feat_ref.shape
    half = own // halves
    row_blocks = dense.shape[0] // bs
    col_blocks = dense.shape[1] // bs
    spots = row_blocks * col_blocks
    row = lax.axis_index("row")
    col = lax.axis_index("col")
    rx, rc = lax.div(row, ri), lax.rem(row, ri)
    cz, cy = lax.div(col, ci), lax.rem(col, ci)

    def remote(src, dst, send, recv, axis, peer):
        return pltpu.make_async_remote_copy(
            src_ref=src,
            dst_ref=dst,
            send_sem=send,
            recv_sem=recv,
            device_id={axis: peer},
            device_id_type=MESH,
        )

    loads = [
        pltpu.make_async_copy(feat_ref, feats.at[row], local_sem.at[0]),
        pltpu.make_async_copy(adj_ref, vals.at[pl.ds(0, slots)], local_sem.at[1]),
        pltpu.make_async_copy(weight_ref, wbuf, local_sem.at[2]),
        pltpu.make_async_copy(gout_ref, gout, local_sem.at[3]),
    ]
    for load in loads:
        load.start()

    barrier = pltpu.get_barrier_semaphore()
    for d in range(1, nrow):
        pl.semaphore_signal(
            barrier, inc=1, device_id={"row": lax.rem(row + d, nrow)}, device_id_type=MESH
        )
    for d in range(1, ncol):
        pl.semaphore_signal(
            barrier, inc=1, device_id={"col": lax.rem(col + d, ncol)}, device_id_type=MESH
        )
    slot = lax.broadcasted_iota(jnp.int32, (spots, slots), 1)
    spot = lax.broadcasted_iota(jnp.int32, (spots, slots), 0)
    hit = (pos_ref[...] == spot) & (slot < count_ref[0, 0])
    found = slots + jnp.sum(jnp.where(hit, slot - slots, 0), axis=1, keepdims=True)
    inv_v[...] = jnp.broadcast_to(found, (spots, 128)).T[:8]
    table = pltpu.make_async_copy(inv_v, inv_s, local_sem.at[4])
    table.start()
    vals[slots] = jnp.zeros((bs, bs), vals.dtype)
    loads[0].wait()
    pl.semaphore_wait(barrier, nrow + ncol - 2)

    g1 = Gather(remote, "row", rx, rc, ro, ri, 1, feats, sem_f, sem_fr)
    g1.start(0)
    table.wait()
    loads[1].wait()

    def fill(r, carry):
        for c in range(col_blocks):
            tile = vals[inv_s[0, r * col_blocks + c]]
            at = pl.ds(pl.multiple_of(r * bs, bs), bs)
            dense[at, c * bs : (c + 1) * bs] = tile
            dense_t[c * bs : (c + 1) * bs, at] = tile.T
        return carry

    lax.fori_loop(0, row_blocks, fill, 0)
    for d in range(1, ro):
        g1.from_outer(0, d)
    for d in range(ro):
        g1.from_inner(0, d)

    def rows(block, h=0, size=own):
        return pl.ds(pl.multiple_of(block * own + h * size, size), size)

    def forward(block, h):
        return jnp.dot(
            dense[rows(block, h, half), :],
            feats[...].reshape(nrow * own, width),
            preferred_element_type=F32,
        )

    line = Line(cz)
    rsc = TreeReduce(
        remote, "col", cz, cy, co, ci, forward, (cs_y, cr_y, cs_z, cr_z), (sem_cy, sem_cz)
    )
    agc = TreeGather(remote, "col", cz, cy, co, ci, halves, ghs, sem_g, sem_gr)
    rsc.line = agc.line = line
    order = [2, 3, 1, 0]
    for h in range(halves):
        for d in order:
            rsc.start(h, d)
    loads[2].wait()
    loads[3].wait()

    def owner(h):
        piece = rsc.end(h).astype(BF16)
        at = slice(h * half, (h + 1) * half)
        af[at, :] = piece
        hidden = jnp.dot(piece, wbuf[...], preferred_element_type=F32)
        sigma = jax.nn.sigmoid(hidden)
        ghs[col * halves + h] = (
            gout[at, :].astype(F32) * sigma * (1.0 + hidden * (1.0 - sigma))
        ).astype(BF16)
        agc.start(h)
        act_ref[at, :] = (hidden * sigma).astype(BF16)

    for h in range(halves):
        for d in order[:-1]:
            rsc.middle(h, d)
        if h:
            owner(h - 1)
        rsc.join(h, 2)
        rsc.join(h, 3)
        rsc.middle(h, 0)
    owner(halves - 1)

    grad = jnp.dot(
        af[...].T,
        ghs[pl.ds(col * halves, halves)].reshape(own, width),
        preferred_element_type=F32,
    )
    rows1 = width // nrow
    rows2 = rows1 // ncol
    ws1[...] = grad.astype(BF16).reshape(nrow, rows1, width)
    w1 = []
    for d in range(1, nrow):
        peer = lax.rem(row + d, nrow)
        copy = remote(
            ws1.at[peer], wr1.at[d - 1], sem_w1.at[0, d - 1], sem_w1.at[1, d - 1], "row", peer
        )
        copy.start()
        w1.append(copy)

    seen = []

    def backward(blocks):
        for block in blocks:
            term = jnp.dot(
                dense_t[:, rows(block)],
                ghs[pl.ds(block * halves, halves)].reshape(own, width),
                preferred_element_type=F32,
            )
            acc[...] = acc[...] + term if seen else term
            seen.append(1)

    last = halves - 1
    for h in range(last):
        for d in range(1, co):
            agc.from_outer(h, d)
    backward([agc.me])

    share = ws1[row].astype(F32)
    for d, copy in enumerate(w1):
        copy.wait_recv()
        share = share + wr1[d].astype(F32)
    for k in range(ncol):
        ws2[k] = share[k * rows2 : (k + 1) * rows2].astype(BF16)
    w2 = []
    for d in range(1, ncol):
        peer = lax.rem(col + d, ncol)
        copy = remote(
            ws2.at[peer], wr2.at[d - 1], sem_w2.at[0, d - 1], sem_w2.at[1, d - 1], "col", peer
        )
        copy.start()
        w2.append(copy)

    arrived = []
    for d in range(1, co):
        arrived += agc.from_outer(last, d)
        if d > 1:
            backward([arrived.pop(0)])
    backward(arrived)

    share = ws2[col].astype(F32)
    for d, copy in enumerate(w2):
        copy.wait_recv()
        share = share + wr2[d].astype(F32)
    w4[row, col] = share.astype(BF16)
    w3 = []
    for d in range(1, ncol):
        peer = lax.rem(col + d, ncol)
        copy = remote(
            w4.at[row, col], w4.at[row, col], sem_w3.at[d - 1], sem_w3r.at[col], "col", peer
        )
        copy.start()
        w3.append(copy)

    for d in range(co):
        for h in range(last):
            agc.from_inner(h, d)
        backward(agc.from_inner(last, d))

    def back(block, h):
        return acc[rows(block, h, half), :]

    rsr = Reduce(
        remote, "row", rx, rc, ro, ri, back, (rs_y, rr_y, rs_z, rr_z), (sem_ry, sem_rz)
    )
    order = list(range(1, ro)) + [0]
    for h in range(halves):
        for d in order:
            rsr.start(h, d)

    for d in range(1, ncol):
        source = lax.rem(col + d, ncol)
        remote(
            w4.at[row, source], w4.at[row, source], sem_w3.at[0], sem_w3r.at[source], "col", source
        ).wait_recv()
    w4c = []
    for d in range(1, nrow):
        peer = lax.rem(row + d, nrow)
        copy = remote(w4.at[row], w4.at[row], sem_w4.at[d - 1], sem_w4r.at[row], "row", peer)
        copy.start()
        w4c.append(copy)

    for h in range(halves):
        for d in order:
            rsr.middle(h, d)
    for d in range(1, nrow):
        source = lax.rem(row + d, nrow)
        remote(
            w4.at[source], w4.at[source], sem_w4.at[0], sem_w4r.at[source], "row", source
        ).wait_recv()
    for r in range(nrow):
        for k in range(ncol):
            at = r * rows1 + k * rows2
            gw_ref[at : at + rows2, :] = w4[r, k].astype(F32)
    for h in range(halves):
        gin_ref[h * half : (h + 1) * half, :] = lax.dot_general(
            rsr.end(h).astype(BF16), wbuf[...], (((1,), (1,)), ((), ())), preferred_element_type=F32
        ).astype(BF16)
    @pl.when(line.central)
    def _():
        for copy in agc.maybe:
            copy.wait_send()

    for copy in g1.sent + rsc.sent + agc.sent + rsr.sent + w1 + w2 + w3 + w4c:
        copy.wait_send()


def hand_on(a_in, b_in, c_in, a_out, b_out, c_out):
    a_out[...] = a_in[...]
    b_out[...] = b_in[...]
    c_out[...] = c_in[...]


def solution(mesh):
    nrow, ncol = mesh.shape["row"], mesh.shape["col"]
    ro, ri = split_axis(nrow, 2)
    co = 4
    ci = ncol // co
    halves = 2
    dims = (nrow, ncol, ro, ri, co, ci, halves)

    def body(features, weight, grad_out, adj_values, block_pos, block_count):
        own, width = features.shape
        slots, bs, _ = adj_values.shape
        rows_tile = own * ncol
        cols_tile = own * nrow
        spots = (rows_tile // bs) * (cols_tile // bs)
        half = own // halves
        rows1 = width // nrow
        rows2 = rows1 // ncol
        dma = pltpu.SemaphoreType.DMA

        def block(n, rows):
            return pltpu.VMEM((max(n, 1), rows, width), BF16)

        def ag_sends(o, i):
            return max((o - 1) + (i - 1) + (o - 1) * (i - 1), 1)

        scratch = [
            pltpu.VMEM((8, spots), jnp.int32),
            pltpu.SMEM((8, spots), jnp.int32),
            pltpu.VMEM((slots + 1, bs, bs), BF16),
            pltpu.VMEM((rows_tile, cols_tile), BF16),
            pltpu.VMEM((cols_tile, rows_tile), BF16),
            block(nrow, own),
            pltpu.VMEM((width, width), BF16),
            pltpu.VMEM((own, width), BF16),
            block(halves * co * (ci - 1), half),
            block(halves * co * (ci - 1), half),
            block(halves * co, half),
            block(halves * co, half),
            pltpu.VMEM((own, width), BF16),
            block(ncol * halves, half),
            pltpu.VMEM((cols_tile, width), F32),
            block(halves * ro * (ri - 1), half),
            block(halves * ro * (ri - 1), half),
            block(halves * (ro - 1), half),
            block(halves * (ro - 1), half),
            block(nrow, rows1),
            block(nrow - 1, rows1),
            block(ncol, rows2),
            block(ncol - 1, rows2),
            pltpu.VMEM((nrow, ncol, rows2, width), BF16),
            dma((5,)),
            dma((ag_sends(ro, ri),)),
            dma((nrow,)),
            dma((2, max(halves * co * (ci - 1), 1))),
            dma((2, halves * co)),
            dma((halves * (ag_sends(co, ci) + 1),)),
            dma((halves * ncol,)),
            dma((2, max(halves * ro * (ri - 1), 1))),
            dma((2, max(halves * (ro - 1), 1))),
            dma((2, nrow)),
            dma((2, ncol)),
            dma((ncol,)),
            dma((ncol,)),
            dma((nrow,)),
            dma((nrow,)),
        ]
        anyspace = pl.BlockSpec(memory_space=pl.ANY)
        vmem = pl.BlockSpec(memory_space=pltpu.VMEM)
        shapes = (
            jax.ShapeDtypeStruct((own, width), BF16),
            jax.ShapeDtypeStruct((own, width), BF16),
            jax.ShapeDtypeStruct((width, width), F32),
        )
        outs = pl.pallas_call(
            functools.partial(kernel, dims),
            out_shape=shapes,
            in_specs=[pl.BlockSpec(memory_space=pltpu.SMEM), vmem] + [anyspace] * 4,
            out_specs=[vmem] * 3,
            scratch_shapes=scratch,
            compiler_params=pltpu.CompilerParams(
                collective_id=0,
                has_side_effects=True,
                vmem_limit_bytes=66 * 1000 * 1000,
            ),
        )(block_count, block_pos, features, weight, grad_out, adj_values)
        return pl.pallas_call(
            hand_on, out_shape=shapes, in_specs=[vmem] * 3, out_specs=[vmem] * 3
        )(*outs)

    placed = (
        P(("col", "row"), None),
        P(),
        P(("row", "col"), None),
        P("row", "col", None),
        P("row", "col"),
        P("row", "col"),
    )
    return jax.shard_map(
        body,
        mesh=mesh,
        in_specs=placed,
        out_specs=(P(("row", "col"), None), P(("col", "row"), None), P()),
        check_vma=False,
    )
```

profile of v0, /device:TPU:0, one launch (start us, length us, event | category | flops | bytes accessed | tf_op | source)
XLA Modules:
  0.0 56.1 jit_solution(13224246349165826145)
XLA Ops:
  1.3 52.9 %shard_map.85 = (bf16[256,256]{1,0:T(8,128)(2,1)}, bf16[256,256]{1,0:T(8,128)(2,1)}, f32[256,256]{1,0:T(8,128)}) custom-call(s32[1,1]{1,0:T(1,128)S(6)} %copy.9.count_ref, s32[1,96]{1,0:T(1,128)} %pos_ref.1, bf16[256,256]{1,0:T(8,128)(2,1)} %feat_ref.1, bf16[256,256]{1,0:T(8,128)(2,1)} %weight_ref.1, bf16[256,256]{1,0:T(8,128)(2,1)} %gout_ref.1, ...), custom_call_target="tpu_custom_call" | custom-call | tf_op jit(solution)/shard_map/pallas_call | solution.py:651
  54.2 1.9 %shard_map.86 = (bf16[256,256]{1,0:T(8,128)(2,1)}, bf16[256,256]{1,0:T(8,128)(2,1)}, f32[256,256]{1,0:T(8,128)}) custom-call(bf16[256,256]{1,0:T(8,128)(2,1)} %get-tuple-element.6.a_in, bf16[256,256]{1,0:T(8,128)(2,1)} %get-tuple-element.7.b_in, f32[256,256]{1,0:T(8,128)} %get-tuple-element.8.c_in), custom_call_target="tpu_custom_call" | custom-call | tf_op jit(solution)/shard_map/pallas_call | solution.py:663
where the time goes:
time: 56.2 us; the launch traced here: 56.1 us
  Pallas kernels  54.8 us (98%)
  between operations  1.29 us (2%)
    pallas_call x1, Pallas kernels, body(): pl.pallas_call(functools.partial(kernel, dims), out_shape=shapes, in_spec...  52.9 us
    pallas_call x1, Pallas kernels, body(): pl.pallas_call(hand_on, out_shape=shapes, in_specs=[vmem] * 3, out_specs=...  1.88 us

commit v1 on v0

v1 whole, which is shorter than its diff:
```python
import functools

import jax
import jax.numpy as jnp
from jax import lax
from jax.experimental import pallas as pl
from jax.experimental.pallas import tpu as pltpu
from jax.sharding import PartitionSpec as P

MESH = pl.DeviceIdType.MESH
F32 = jnp.float32
BF16 = jnp.bfloat16
OWN, MATE, NEAR, FAR = 0, 1, 2, 3
END_LAG = 0.5
W_GAPS = (0.3, 3.6, 4.5)


def split_axis(size, inner):
    while size % inner:
        inner -= 1
    return size // inner, inner


def send_order(parts):
    first = [(0, d) for d in (NEAR, FAR, MATE, OWN)]
    far = [(q, d) for q in range(1, parts) for d in (NEAR, FAR)]
    close = [(q, d) for q in range(1, parts) for d in (MATE, OWN)]
    return first + far + close


def plan(parts, order, ci):
    wire, hop, line, extra, work = 2.8 / parts, 1.7, 2.2, 0.8, 0.4
    step = wire + line
    y = {at: 0.4 + wire * (k + 1) + hop for k, at in enumerate(order)}
    events, ready = [], {"rim": [], "cen": []}
    ends = 0.0
    for q in range(parts):
        rim = {d: y[q, d] for d in (NEAR, FAR, MATE)}
        for d in (NEAR, FAR, MATE):
            events.append((rim[d], "rim", "M", q, d))
        events.append((y[q, MATE], "cen", "M", q, MATE))
        join = {d: max(y[q, d], rim[d] + step) for d in (NEAR, FAR)}
        for d in (NEAR, FAR):
            events.append((join[d], "cen", "J", q, d))
        cen = max(y[q, OWN], rim[MATE] + step, join[NEAR] + step) + END_LAG
        out = max(y[q, OWN], y[q, MATE] + step, join[FAR] + step + extra) + END_LAG
        events.append((cen, "cen", "E", q, OWN))
        events.append((out, "rim", "E", q, OWN))
        cen, out = cen + work, out + work
        ends = max(ends, cen, out)
        at_cen = {OWN: cen, NEAR: cen + step, MATE: out + step + wire, FAR: out + step + extra}
        at_rim = {
            OWN: out,
            MATE: cen + step + wire,
            NEAR: at_cen[NEAR] + step,
            FAR: at_cen[FAR] + step,
        }
        for d in (MATE, NEAR, FAR):
            events.append((at_cen[d], "cen", "O", q, d))
            events.append((at_rim[d], "rim", "O", q, d))
        ready["cen"] += [(at_cen[d], q, d) for d in range(4)]
        ready["rim"] += [(at_rim[d], q, d) for d in range(4)]
    there = {}
    for role, pieces in ready.items():
        free = 0.4 + wire * len(order)
        for when, q, d in sorted(pieces):
            free = max(free, when) + wire
            there[d] = max(there.get(d, 0.0), free + hop)
    blocks = []
    for d in range(4):
        here = max(when for role in ready for when, _, at in ready[role] if at == d)
        blocks.append((here + 0.01, d, 0))
        for e in range(1, ci):
            blocks.append((there[d] + 0.01 * e, d, e))
    blocks.sort()
    for when, d, e in blocks[:-1]:
        events.append((when, "all", "B", d, e))
    for k, gap in enumerate(W_GAPS):
        ends += gap
        events.append((ends, "all", "W", k, 0))
    events.append((y[0, NEAR] + 0.02, "all", "P", MATE, 0))
    events.append((y[0, FAR] + 0.02, "all", "P", OWN, 0))
    events.sort(key=lambda event: event[0])
    return events, blocks[-1][1:]


def kernel(
    dims,
    count_ref,
    pos_ref,
    feat_ref,
    weight_ref,
    gout_ref,
    adj_ref,
    act_ref,
    gin_ref,
    gw_ref,
    pos_v,
    inv_v,
    inv_s,
    vals,
    dense,
    dense_t,
    feats,
    pair,
    mine,
    s_in,
    r_in,
    s_out,
    r_out,
    af,
    ghs,
    acc,
    rs_y,
    rr_y,
    rs_z,
    rr_z,
    ws1,
    wr1,
    ws2,
    wr2,
    w4,
    local_sem,
    sem_sent,
    sem_fx,
    sem_fs,
    sem_c,
    sem_a,
    sem_b,
    sem_ry,
    sem_r0,
    sem_rz,
    sem_w,
):
    (nrow, ncol, ro, ri, co, ci, parts) = dims
    slots, bs, _ = adj_ref.shape
    own, width = feat_ref.shape
    piece = own // parts
    row_blocks = dense.shape[0] // bs
    col_blocks = dense.shape[1] // bs
    spots = row_blocks * col_blocks
    row = lax.axis_index("row")
    col = lax.axis_index("col")
    rx, rc = lax.div(row, ri), lax.rem(row, ri)
    cz, cy = lax.div(col, ci), lax.rem(col, ci)

    def remote(src, dst, send, recv, axis, peer):
        return pltpu.make_async_remote_copy(
            src_ref=src,
            dst_ref=dst,
            send_sem=send,
            recv_sem=recv,
            device_id={axis: peer},
            device_id_type=MESH,
        )

    loads = [
        pltpu.make_async_copy(feat_ref, feats.at[row], local_sem.at[0]),
        pltpu.make_async_copy(pos_ref, pos_v, local_sem.at[3]),
        pltpu.make_async_copy(adj_ref, vals.at[pl.ds(0, slots)], local_sem.at[1]),
        pltpu.make_async_copy(weight_ref, pair.at[0], local_sem.at[2]),
        pltpu.make_async_copy(gout_ref, pair.at[1], local_sem.at[2]),
    ]
    for load in loads:
        load.start()

    barrier = pltpu.get_barrier_semaphore()
    for d in range(1, nrow):
        pl.semaphore_signal(
            barrier, inc=1, device_id={"row": lax.rem(row + d, nrow)}, device_id_type=MESH
        )
    for d in range(1, ncol):
        pl.semaphore_signal(
            barrier, inc=1, device_id={"col": lax.rem(col + d, ncol)}, device_id_type=MESH
        )
    vals[slots] = jnp.zeros((bs, bs), vals.dtype)
    loads[1].wait()
    slot = lax.broadcasted_iota(jnp.int32, (spots, slots), 1)
    spot = lax.broadcasted_iota(jnp.int32, (spots, slots), 0)
    hit = (pos_v[...] == spot) & (slot < count_ref[0, 0])
    found = slots + jnp.sum(jnp.where(hit, slot - slots, 0), axis=1, keepdims=True)
    inv_v[...] = jnp.broadcast_to(found, (spots, 128)).T[:8]
    table = pltpu.make_async_copy(inv_v, inv_s, local_sem.at[4])
    table.start()
    loads[0].wait()
    pl.semaphore_wait(barrier, nrow + ncol - 2)

    halves = 2
    half = own // halves

    def feature(block, h, sem, peer):
        at = feats.at[block, pl.ds(h * half, half)]
        return remote(at, at, sem_sent.at[0], sem, "row", peer)

    def feature_x(block, h, d):
        sem = sem_fx.at[(ro - d - 1) * halves + h]
        return feature(block, h, sem, lax.rem(rx + d, ro) * ri + rc)

    def feature_in(block, h):
        for e in range(1, ri):
            feature(block, h, sem_fs.at[0], rx * ri + lax.rem(rc + e, ri)).start()

    for h in range(halves):
        for d in range(1, ro):
            feature_x(row, h, d).start()
    for h in range(halves):
        feature_in(row, h)
    table.wait()
    loads[2].wait()

    def fill(r, carry):
        for c in range(col_blocks):
            tile = vals[inv_s[0, r * col_blocks + c]]
            at = pl.ds(pl.multiple_of(r * bs, bs), bs)
            dense[at, c * bs : (c + 1) * bs] = tile
            dense_t[c * bs : (c + 1) * bs, at] = tile.T
        return carry

    lax.fori_loop(0, row_blocks, fill, 0)
    for h in range(halves):
        for d in range(1, ro):
            block = lax.rem(rx + d, ro) * ri + rc
            feature_x(block, h, ro - d).wait_recv()
            feature_in(block, h)
    if ri > 1:
        at = feats.at[pl.ds(0, ro * (ri - 1))]
        remote(at, at, sem_sent.at[0], sem_fs.at[0], "row", 0).wait_recv()

    def rows(block, size=own):
        return pl.ds(pl.multiple_of(block * size, size), size)

    def forward(block):
        return jnp.dot(
            dense[rows(block), :],
            feats[...].reshape(nrow * own, width),
            preferred_element_type=F32,
        )

    central = lax.rem(lax.div(cz + 1, 2), 2) == 1
    mate = cz + 1 - 2 * lax.rem(cz, 2)
    near = 2 - lax.div(cz, 2)
    place = (cz, mate, near, 3 * (near - 1))

    def cut(q):
        return pl.ds(q * piece, piece)

    def pieces(n, sem):
        at = r_out.at[pl.ds(0, n)]
        remote(at, at, sem_sent.at[0], sem, "col", 0).wait_recv()

    def inner_copy(q, d, e):
        at = d * (ci - 1) + e - 1
        return remote(
            s_in.at[at, cut(q)],
            r_in.at[at, cut(q)],
            sem_sent.at[0],
            sem_c.at[q * 4 + d],
            "col",
            cz * ci + lax.rem(cy + e, ci),
        )

    order = send_order(parts)
    queue = list(order)
    done = set()
    for d in (NEAR, FAR, MATE, OWN):
        for e in range(1, ci):
            s_in[d * (ci - 1) + e - 1] = forward(place[d] * ci + lax.rem(cy + e, ci)).astype(BF16)
        done.add(d)
        while queue and queue[0][1] in done and (queue[0][0] == 0 or len(done) == co):
            for e in range(1, ci):
                inner_copy(*queue[0], e).start()
            queue.pop(0)

    def own_part(d):
        mine[d] = forward(place[d] * ci + cy)

    own_part(NEAR)
    own_part(FAR)
    pltpu.make_async_copy(pair, pair, local_sem.at[2]).wait()

    def joined(q, d, others=()):
        n = ci - 1 + len(others)
        if n:
            pieces(n, sem_c.at[q * 4 + d])
        value = mine[d, cut(q)]
        for e in range(1, ci):
            value = value + r_in[d * (ci - 1) + e - 1, cut(q)].astype(F32)
        for landing in others:
            value = value + r_out[q * 4 + landing].astype(F32)
        return value

    def hop(q, d, landing, peer):
        return remote(
            s_out.at[q * 4 + d],
            r_out.at[q * 4 + landing],
            sem_sent.at[0],
            sem_c.at[q * 4 + (landing if landing > 1 else OWN)],
            "col",
            peer * ci + cy,
        )

    def push(block, q, sem, peer):
        at = ghs.at[block, cut(q)]
        return remote(at, at, sem_sent.at[0], sem, "col", peer)

    def inward(block, q, d):
        for e in range(1, ci):
            sem = sem_b.at[d * (ci - 1) + ci - e - 1]
            push(block, q, sem, cz * ci + lax.rem(cy + e, ci)).start()

    def middle(q, d):
        s_out[q * 4 + d] = joined(q, d).astype(BF16)
        hop(q, d, 0 if d == MATE else d, mate).start()

    def join(q, d):
        s_out[q * 4 + d] = joined(q, d, (d,)).astype(BF16)
        hop(q, d, 1, place[d]).start()

    def end(q, role):
        part = joined(q, OWN, (0, 1)).astype(BF16)
        af[cut(q), :] = part
        hidden = jnp.dot(part, pair[0], preferred_element_type=F32)
        sigma = jax.nn.sigmoid(hidden)
        ghs[col, cut(q)] = (
            pair[1, cut(q)].astype(F32) * sigma * (1.0 + hidden * (1.0 - sigma))
        ).astype(BF16)
        label = NEAR if role == "cen" else FAR
        push(col, q, sem_a.at[q * 3 + label - 1], near * ci + cy).start()
        push(col, q, sem_a.at[q * 3 + MATE - 1], mate * ci + cy).start()
        inward(col, q, OWN)
        act_ref[cut(q), :] = (hidden * sigma).astype(BF16)

    def outer(q, d, role):
        block = place[d] * ci + cy
        push(block, q, sem_a.at[q * 3 + d - 1], 0).wait_recv()
        if role == "cen" and d > 1:
            push(block, q, sem_a.at[q * 3 + d - 1], mate * ci + cy).start()
        inward(block, q, d)

    seen = []

    def gathered(d, e):
        block = place[d] * ci + lax.rem(cy + e, ci)
        if e:
            at = ghs.at[block]
            remote(at, at, sem_sent.at[0], sem_b.at[d * (ci - 1) + e - 1], "col", 0).wait_recv()
        return block

    def backward(d, e):
        block = gathered(d, e)
        term = jnp.dot(dense_t[:, rows(block)], ghs[block], preferred_element_type=F32)
        acc[...] = acc[...] + term if seen else term
        seen.append(1)

    rows1 = width // nrow
    rows2 = rows1 // ncol

    def w_send(k, source, target, axis, peer):
        remote(source, target, sem_w.at[0, k], sem_w.at[1, k], axis, peer).start()

    w_refs = (wr1, wr2, w4.at[0, pl.ds(0, nrow - 1)], w4.at[pl.ds(0, ncol - 1)])

    def w_copy(k):
        return remote(w_refs[k], w_refs[k], sem_w.at[0, k], sem_w.at[1, k], "col", 0)

    def weight_step(k):
        if k == 0:
            grad = jnp.dot(af[...].T, ghs[col], preferred_element_type=F32)
            ws1[...] = grad.astype(BF16).reshape(nrow, rows1, width)
            for d in range(1, nrow):
                peer = lax.rem(row + d, nrow)
                w_send(0, ws1.at[peer], wr1.at[d - 1], "row", peer)
        elif k == 1:
            w_copy(0).wait_recv()
            share = ws1[row].astype(F32)
            for d in range(1, nrow):
                share = share + wr1[d - 1].astype(F32)
            for j in range(ncol):
                ws2[j] = share[j * rows2 : (j + 1) * rows2].astype(BF16)
            for d in range(1, ncol):
                peer = lax.rem(col + d, ncol)
                w_send(1, ws2.at[peer], wr2.at[d - 1], "col", peer)
        elif k == 2:
            w_copy(1).wait_recv()
            share = ws2[col].astype(F32)
            for d in range(1, ncol):
                share = share + wr2[d - 1].astype(F32)
            w4[col, row] = share.astype(BF16)
            for d in range(1, nrow):
                at = w4.at[col, row]
                w_send(2, at, at, "row", lax.rem(row + d, nrow))
        elif k == 3:
            w_copy(2).wait_recv()
            for d in range(1, ncol):
                w_send(3, w4.at[col], w4.at[col], "col", lax.rem(col + d, ncol))
        else:
            w_copy(3).wait_recv()
            for r in range(nrow):
                for k in range(ncol):
                    at = r * rows1 + k * rows2
                    gw_ref[at : at + rows2, :] = w4[k, r].astype(F32)

    def act_on(event, role):
        _, _, kind, a, b = event
        if kind == "M":
            middle(a, b)
        elif kind == "J":
            join(a, b)
        elif kind == "E":
            end(a, role)
        elif kind == "O":
            outer(a, b, role)
        elif kind == "B":
            backward(a, b)
        elif kind == "P":
            own_part(a)
        else:
            weight_step(a)

    events, final = plan(parts, order, ci)
    pending = {"rim": [], "cen": []}

    def flush():
        for role, here in (("cen", central), ("rim", jnp.logical_not(central))):
            todo = pending[role]
            pending[role] = []
            if todo:

                @pl.when(here)
                def _():
                    for event in todo:
                        act_on(event, role)

    for event in events:
        if event[1] == "all":
            flush()
            act_on(event, "all")
        else:
            pending[event[1]].append(event)
    flush()

    block = gathered(*final)
    last = ghs[block]

    def finished(to, core):
        at = rows(to * ri + core)
        return acc[at, :] + jnp.dot(
            dense_t[at, rows(block)], last, preferred_element_type=F32
        )

    def sibling(d, e, p):
        at = d * (ri - 1) + e - 1
        return remote(
            rs_y.at[at, cut(p)],
            rr_y.at[at, cut(p)],
            sem_sent.at[0],
            sem_ry.at[(d - 1) * parts + p] if d else sem_r0.at[0],
            "row",
            rx * ri + lax.rem(rc + e, ri),
        )

    def across(d, p):
        return remote(
            rs_z.at[d - 1, cut(p)],
            rr_z.at[d - 1, cut(p)],
            sem_sent.at[0],
            sem_rz.at[(d - 1) * parts + p],
            "row",
            lax.rem(rx + d, ro) * ri + rc,
        )

    targets = list(range(1, ro)) + [0]
    for d in targets:
        to = lax.rem(rx + d, ro)
        for e in range(1, ri):
            rs_y[d * (ri - 1) + e - 1] = finished(to, lax.rem(rc + e, ri)).astype(BF16)
            for p in range(parts):
                sibling(d, e, p).start()
    for d in targets:
        at = rows(lax.rem(rx + d, ro) * ri + rc)
        acc[at, :] = finished(lax.rem(rx + d, ro), rc)

    def chip_sum(d, p):
        at = pl.ds(pl.multiple_of((lax.rem(rx + d, ro) * ri + rc) * own + p * piece, piece), piece)
        value = acc[at, :]
        for e in range(1, ri):
            value = value + rr_y[d * (ri - 1) + e - 1, cut(p)].astype(F32)
        return value

    for p in range(parts):
        for d in range(1, ro):
            if ri > 1:
                pieces(ri - 1, sem_ry.at[(d - 1) * parts + p])
            rs_z[d - 1, cut(p)] = chip_sum(d, p).astype(BF16)
            across(d, p).start()
    weight_step(3)
    if ri > 1:
        at = rr_y.at[pl.ds(0, ri - 1)]
        remote(at, at, sem_sent.at[0], sem_r0.at[0], "row", 0).wait_recv()
    for p in range(parts):
        value = chip_sum(0, p)
        for d in range(1, ro):
            across(d, p).wait_recv()
            value = value + rr_z[d - 1, cut(p)].astype(F32)
        gin_ref[cut(p), :] = lax.dot_general(
            value.astype(BF16), pair[0], (((1,), (1,)), ((), ())), preferred_element_type=F32
        ).astype(BF16)
    weight_step(4)

    def all_sent(extra):
        blocks = (ro - 1) + ro * (ri - 1)
        blocks += co * (ci - 1) + (co - 1) + 2 + co * (ci - 1) + extra
        blocks += ro * (ri - 1) + (ro - 1)
        at = dense.at[pl.ds(0, blocks * own * width // dense.shape[1])]
        remote(at, at, sem_sent.at[0], sem_sent.at[0], "row", 0).wait_send()

    @pl.when(central)
    def _():
        all_sent(2)

    @pl.when(jnp.logical_not(central))
    def _():
        all_sent(0)

    for k in range(4):
        w_copy(k).wait_send()


def hand_on(a_in, b_in, c_in, a_out, b_out, c_out, sems):
    copies = [
        pltpu.make_async_copy(source, target, sems.at[k])
        for k, (source, target) in enumerate(((a_in, a_out), (b_in, b_out), (c_in, c_out)))
    ]
    for copy in copies:
        copy.start()
    for copy in copies:
        copy.wait()


def solution(mesh):
    nrow, ncol = mesh.shape["row"], mesh.shape["col"]
    ro, ri = split_axis(nrow, 2)
    co = 4
    ci = ncol // co
    parts = 4
    dims = (nrow, ncol, ro, ri, co, ci, parts)

    def body(features, weight, grad_out, adj_values, block_pos, block_count):
        own, width = features.shape
        slots, bs, _ = adj_values.shape
        rows_tile = own * ncol
        cols_tile = own * nrow
        spots = (rows_tile // bs) * (cols_tile // bs)
        piece = own // parts
        rows1 = width // nrow
        rows2 = rows1 // ncol
        dma = pltpu.SemaphoreType.DMA

        def block(n, rows, dtype=BF16):
            return pltpu.VMEM((max(n, 1), rows, width), dtype)

        scratch = [
            pltpu.VMEM((1, slots), jnp.int32),
            pltpu.VMEM((8, spots), jnp.int32),
            pltpu.SMEM((8, spots), jnp.int32),
            pltpu.VMEM((slots + 1, bs, bs), BF16),
            pltpu.VMEM((rows_tile, cols_tile), BF16),
            pltpu.VMEM((cols_tile, rows_tile), BF16),
            block(nrow, own),
            block(2, own),
            block(co, own, F32),
            block(co * (ci - 1), own),
            block(co * (ci - 1), own),
            block(parts * 4, piece),
            block(parts * 4, piece),
            pltpu.VMEM((own, width), BF16),
            block(ncol, own),
            pltpu.VMEM((cols_tile, width), F32),
            block(ro * (ri - 1), own),
            block(ro * (ri - 1), own),
            block(ro - 1, own),
            block(ro - 1, own),
            block(nrow, rows1),
            block(nrow - 1, rows1),
            block(ncol, rows2),
            block(ncol - 1, rows2),
            pltpu.VMEM((ncol, nrow, rows2, width), BF16),
            dma((5,)),
            dma((1,)),
            dma((max(2 * (ro - 1), 1),)),
            dma((1,)),
            dma((parts * 4,)),
            dma((parts * 3,)),
            dma((max(co * (ci - 1), 1),)),
            dma((max(parts * (ro - 1), 1),)),
            dma((1,)),
            dma((max(parts * (ro - 1), 1),)),
            dma((2, 4)),
        ]
        vmem = pl.BlockSpec(memory_space=pltpu.VMEM)
        anyspace = pl.BlockSpec(memory_space=pl.ANY)
        shapes = (
            jax.ShapeDtypeStruct((own, width), BF16),
            jax.ShapeDtypeStruct((own, width), BF16),
            jax.ShapeDtypeStruct((width, width), F32),
        )
        held = sum(
            2 * ref.dtype.itemsize * functools.reduce(lambda a, b: a * b, ref.shape, 1) // 2
            for ref in scratch
            if getattr(ref, "memory_space", None) == pltpu.VMEM
        )
        outs = pl.pallas_call(
            functools.partial(kernel, dims),
            out_shape=shapes,
            in_specs=[pl.BlockSpec(memory_space=pltpu.SMEM)] + [anyspace] * 5,
            out_specs=[vmem] * 3,
            scratch_shapes=scratch,
            compiler_params=pltpu.CompilerParams(
                collective_id=0,
                has_side_effects=True,
                vmem_limit_bytes=min(held + (6 << 20), 66 * 1000 * 1000),
            ),
        )(
            block_count,
            *(
                pltpu.with_memory_space_constraint(x, pltpu.HBM)
                for x in (block_pos, features, weight, grad_out, adj_values)
            ),
        )
        return pl.pallas_call(
            hand_on,
            out_shape=shapes,
            in_specs=[anyspace] * 3,
            out_specs=[anyspace] * 3,
            scratch_shapes=[dma((3,))],
            compiler_params=pltpu.CompilerParams(vmem_limit_bytes=1 << 20),
        )(*outs)

    placed = (
        P(("col", "row"), None),
        P(),
        P(("row", "col"), None),
        P("row", "col", None),
        P("row", "col"),
        P("row", "col"),
    )
    return jax.shard_map(
        body,
        mesh=mesh,
        in_specs=placed,
        out_specs=(P(("row", "col"), None), P(("col", "row"), None), P()),
        check_vma=False,
    )
```

time: 56.2 us -> 47.8 us (0.85)
  Pallas kernels: 54.8 us -> 46.4 us
    pallas_call x1, Pallas kernels: 52.9 us -> 45.6 us  [body(): pl.pallas_call(functools.partial(kernel, dims), out_shape=shapes, in_spec...]
    pallas_call x1, Pallas kernels: 1.88 us -> 0.82 us  [body(): pl.pallas_call(hand_on, out_shape=shapes, in_specs=[anyspace] * 3, out_sp...]
where the time goes in v1:
time: 47.8 us; the launch traced here: 47.7 us
  Pallas kernels  46.4 us (97%)
  between operations  1.29 us (3%)
    pallas_call x1, Pallas kernels, body(): pl.pallas_call(functools.partial(kernel, dims), out_shape=shapes, in_spec...  45.6 us

profile of v1, /device:TPU:0, one launch (start us, length us, event | category | flops | bytes accessed | tf_op | source)
XLA Modules:
  0.0 47.7 jit_solution(8665161493229976583)
XLA Ops:
  1.3 45.6 %shard_map.85 = (bf16[256,256]{1,0:T(8,128)(2,1)S(1)}, bf16[256,256]{1,0:T(8,128)(2,1)S(1)}, f32[256,256]{1,0:T(8,128)S(1)}) custom-call(s32[1,1]{1,0:T(1,128)S(6)} %copy.9.count_ref, s32[1,96]{1,0:T(1,128)} %pos_ref.1, bf16[256,256]{1,0:T(8,128)(2,1)} %feat_ref.1, bf16[256,256]{1,0:T(8,128)(2,1)} %weight_ref.1, bf16[256,256]{1,0:T(8,128)(2,1)} %gout_ref.1, ...), custom_call_target="tpu_custom_call" | custom-call | tf_op jit(solution)/shard_map/pallas_call | solution.py:612
  46.9 0.8 %shard_map.86 = (bf16[256,256]{1,0:T(8,128)(2,1)}, bf16[256,256]{1,0:T(8,128)(2,1)}, f32[256,256]{1,0:T(8,128)}) custom-call(bf16[256,256]{1,0:T(8,128)(2,1)S(1)} %get-tuple-element.6.a_in, bf16[256,256]{1,0:T(8,128)(2,1)S(1)} %get-tuple-element.7.b_in, f32[256,256]{1,0:T(8,128)S(1)} %get-tuple-element.8.c_in), custom_call_target="tpu_custom_call" | custom-call | tf_op jit(solution)/shard_map/pallas_call | solution.py:630

commit v2 on v1

--- a/solution.py
+++ b/solution.py
@@ -11,77 +11,37 @@
 F32 = jnp.float32
 BF16 = jnp.bfloat16
 OWN, MATE, NEAR, FAR = 0, 1, 2, 3
-END_LAG = 0.5
-W_GAPS = (0.3, 3.6, 4.5)
+PARTS = 4
+ORDER = (
+    (0, 2), (0, 3), (2, 3), (1, 3), (1, 2), (0, 1), (3, 3), (3, 2),
+    (2, 2), (3, 1), (1, 1), (2, 1), (0, 0), (1, 0), (2, 0), (3, 0),
+)
+RIM = (
+    ("P", 2, 0), ("P", 3, 0), ("P", 1, 0), ("M", 0, 2), ("P", 0, 0), ("M", 0, 3),
+    ("M", 2, 3), ("M", 1, 3), ("M", 1, 2), ("M", 0, 1), ("M", 3, 3), ("M", 3, 2),
+    ("M", 2, 2), ("M", 3, 1), ("M", 1, 1), ("M", 2, 1), ("E", 0, 0), ("E", 1, 0),
+    ("E", 2, 0), ("E", 3, 0), ("W", 0, 0), ("B", 0, 0), ("O", 0, 1), ("O", 1, 1),
+    ("O", 3, 1), ("O", 0, 2), ("W", 1, 0), ("O", 2, 1), ("B", 1, 0), ("O", 0, 3),
+    ("O", 1, 2), ("O", 3, 2), ("O", 1, 3), ("O", 2, 2), ("B", 2, 0), ("O", 2, 3),
+    ("O", 3, 3), ("B", 3, 0), ("B", 0, 1), ("B", 1, 1), ("W", 2, 0), ("B", 2, 1),
+    ("B", 3, 1),
+)
+CENTRAL = (
+    ("P", 2, 0), ("P", 3, 0), ("P", 1, 0), ("P", 0, 0), ("J", 0, 2), ("M", 0, 1),
+    ("J", 0, 3), ("J", 2, 3), ("J", 1, 3), ("J", 1, 2), ("M", 3, 1), ("M", 1, 1),
+    ("J", 3, 3), ("M", 2, 1), ("J", 3, 2), ("E", 0, 0), ("J", 2, 2), ("E", 1, 0),
+    ("E", 3, 0), ("O", 0, 2), ("O", 0, 1), ("E", 2, 0), ("W", 0, 0), ("B", 0, 0),
+    ("O", 0, 3), ("O", 1, 2), ("O", 1, 1), ("O", 3, 2), ("O", 1, 3), ("O", 2, 1),
+    ("O", 2, 2), ("W", 1, 0), ("B", 2, 0), ("O", 2, 3), ("O", 3, 1), ("B", 1, 0),
+    ("O", 3, 3), ("B", 3, 0), ("B", 0, 1), ("B", 2, 1), ("W", 2, 0), ("B", 1, 1),
+    ("B", 3, 1),
+)
 
 
 def split_axis(size, inner):
     while size % inner:
         inner -= 1
     return size // inner, inner
-
-
-def send_order(parts):
-    first = [(0, d) for d in (NEAR, FAR, MATE, OWN)]
-    far = [(q, d) for q in range(1, parts) for d in (NEAR, FAR)]
-    close = [(q, d) for q in range(1, parts) for d in (MATE, OWN)]
-    return first + far + close
-
-
-def plan(parts, order, ci):
-    wire, hop, line, extra, work = 2.8 / parts, 1.7, 2.2, 0.8, 0.4
-    step = wire + line
-    y = {at: 0.4 + wire * (k + 1) + hop for k, at in enumerate(order)}
-    events, ready = [], {"rim": [], "cen": []}
-    ends = 0.0
-    for q in range(parts):
-        rim = {d: y[q, d] for d in (NEAR, FAR, MATE)}
-        for d in (NEAR, FAR, MATE):
-            events.append((rim[d], "rim", "M", q, d))
-        events.append((y[q, MATE], "cen", "M", q, MATE))
-        join = {d: max(y[q, d], rim[d] + step) for d in (NEAR, FAR)}
-        for d in (NEAR, FAR):
-            events.append((join[d], "cen", "J", q, d))
-        cen = max(y[q, OWN], rim[MATE] + step, join[NEAR] + step) + END_LAG
-        out = max(y[q, OWN], y[q, MATE] + step, join[FAR] + step + extra) + END_LAG
-        events.append((cen, "cen", "E", q, OWN))
-        events.append((out, "rim", "E", q, OWN))
-        cen, out = cen + work, out + work
-        ends = max(ends, cen, out)
-        at_cen = {OWN: cen, NEAR: cen + step, MATE: out + step + wire, FAR: out + step + extra}
-        at_rim = {
-            OWN: out,
-            MATE: cen + step + wire,
-            NEAR: at_cen[NEAR] + step,
-            FAR: at_cen[FAR] + step,
-        }
-        for d in (MATE, NEAR, FAR):
-            events.append((at_cen[d], "cen", "O", q, d))
-            events.append((at_rim[d], "rim", "O", q, d))
-        ready["cen"] += [(at_cen[d], q, d) for d in range(4)]
-        ready["rim"] += [(at_rim[d], q, d) for d in range(4)]
-    there = {}
-    for role, pieces in ready.items():
-        free = 0.4 + wire * len(order)
-        for when, q, d in sorted(pieces):
-            free = max(free, when) + wire
-            there[d] = max(there.get(d, 0.0), free + hop)
-    blocks = []
-    for d in range(4):
-        here = max(when for role in ready for when, _, at in ready[role] if at == d)
-        blocks.append((here + 0.01, d, 0))
-        for e in range(1, ci):
-            blocks.append((there[d] + 0.01 * e, d, e))
-    blocks.sort()
-    for when, d, e in blocks[:-1]:
-        events.append((when, "all", "B", d, e))
-    for k, gap in enumerate(W_GAPS):
-        ends += gap
-        events.append((ends, "all", "W", k, 0))
-    events.append((y[0, NEAR] + 0.02, "all", "P", MATE, 0))
-    events.append((y[0, FAR] + 0.02, "all", "P", OWN, 0))
-    events.sort(key=lambda event: event[0])
-    return events, blocks[-1][1:]
 
 
 def kernel(
@@ -121,6 +81,7 @@
     wr2,
     w4,
     local_sem,
+    sem_up,
     sem_sent,
     sem_fx,
     sem_fs,
@@ -161,7 +122,7 @@
         pltpu.make_async_copy(weight_ref, pair.at[0], local_sem.at[2]),
         pltpu.make_async_copy(gout_ref, pair.at[1], local_sem.at[2]),
     ]
-    for load in loads:
+    for load in loads[:2]:
         load.start()
 
     barrier = pltpu.get_barrier_semaphore()
@@ -169,10 +130,23 @@
         pl.semaphore_signal(
             barrier, inc=1, device_id={"row": lax.rem(row + d, nrow)}, device_id_type=MESH
         )
-    for d in range(1, ncol):
+    for e in range(1, ci):
         pl.semaphore_signal(
-            barrier, inc=1, device_id={"col": lax.rem(col + d, ncol)}, device_id_type=MESH
-        )
+            barrier, inc=1, device_id={"col": cz * ci + lax.rem(cy + e, ci)}, device_id_type=MESH
+        )
+
+    def greet(sem, d):
+        at = cz + d
+
+        @pl.when((at >= 0) & (at < co))
+        def _():
+            for e in range(ci):
+                pl.semaphore_signal(
+                    sem, inc=1, device_id={"col": at * ci + e}, device_id_type=MESH
+                )
+
+    for d in range(1, co):
+        greet(barrier, d)
     vals[slots] = jnp.zeros((bs, bs), vals.dtype)
     loads[1].wait()
     slot = lax.broadcasted_iota(jnp.int32, (spots, slots), 1)
@@ -183,7 +157,11 @@
     table = pltpu.make_async_copy(inv_v, inv_s, local_sem.at[4])
     table.start()
     loads[0].wait()
-    pl.semaphore_wait(barrier, nrow + ncol - 2)
+    for load in loads[2:]:
+        load.start()
+    pl.semaphore_wait(barrier, nrow - 1 + ci - 1 + cz * ci)
+    for d in range(1, co):
+        greet(sem_up, -d)
 
     halves = 2
     half = own // halves
@@ -259,23 +237,24 @@
             cz * ci + lax.rem(cy + e, ci),
         )
 
-    order = send_order(parts)
-    queue = list(order)
-    done = set()
-    for d in (NEAR, FAR, MATE, OWN):
-        for e in range(1, ci):
-            s_in[d * (ci - 1) + e - 1] = forward(place[d] * ci + lax.rem(cy + e, ci)).astype(BF16)
-        done.add(d)
-        while queue and queue[0][1] in done and (queue[0][0] == 0 or len(done) == co):
+    def partial(targets, queue):
+        done = []
+        queue = list(queue)
+        for d in targets:
             for e in range(1, ci):
-                inner_copy(*queue[0], e).start()
-            queue.pop(0)
+                block = place[d] * ci + lax.rem(cy + e, ci)
+                s_in[d * (ci - 1) + e - 1] = forward(block).astype(BF16)
+            done.append(d)
+            while queue and (queue[0][1] in done or d == targets[-1]):
+                for e in range(1, ci):
+                    inner_copy(*queue[0], e).start()
+                queue.pop(0)
+
+    partial((NEAR, FAR, MATE, OWN), ORDER)
 
     def own_part(d):
         mine[d] = forward(place[d] * ci + cy)
 
-    own_part(NEAR)
-    own_part(FAR)
     pltpu.make_async_copy(pair, pair, local_sem.at[2]).wait()
 
     def joined(q, d, others=()):
@@ -337,7 +316,7 @@
             push(block, q, sem_a.at[q * 3 + d - 1], mate * ci + cy).start()
         inward(block, q, d)
 
-    seen = []
+    final = FAR, ci - 1
 
     def gathered(d, e):
         block = place[d] * ci + lax.rem(cy + e, ci)
@@ -346,11 +325,14 @@
             remote(at, at, sem_sent.at[0], sem_b.at[d * (ci - 1) + e - 1], "col", 0).wait_recv()
         return block
 
-    def backward(d, e):
-        block = gathered(d, e)
-        term = jnp.dot(dense_t[:, rows(block)], ghs[block], preferred_element_type=F32)
-        acc[...] = acc[...] + term if seen else term
-        seen.append(1)
+    def backward(d, others, seen):
+        for e in range(1, ci) if others else (0,):
+            if (d, e) == final:
+                continue
+            block = gathered(d, e)
+            term = jnp.dot(dense_t[:, rows(block)], ghs[block], preferred_element_type=F32)
+            acc[...] = acc[...] + term if seen else term
+            seen.append(1)
 
     rows1 = width // nrow
     rows2 = rows1 // ncol
@@ -400,8 +382,8 @@
                     at = r * rows1 + k * rows2
                     gw_ref[at : at + rows2, :] = w4[k, r].astype(F32)
 
-    def act_on(event, role):
-        _, _, kind, a, b = event
+    def act_on(event, role, seen):
+        kind, a, b = event
         if kind == "M":
             middle(a, b)
         elif kind == "J":
@@ -411,33 +393,28 @@
         elif kind == "O":
             outer(a, b, role)
         elif kind == "B":
-            backward(a, b)
+            backward(a, b, seen)
         elif kind == "P":
             own_part(a)
         else:
             weight_step(a)
 
-    events, final = plan(parts, order, ci)
-    pending = {"rim": [], "cen": []}
-
-    def flush():
-        for role, here in (("cen", central), ("rim", jnp.logical_not(central))):
-            todo = pending[role]
-            pending[role] = []
-            if todo:
-
-                @pl.when(here)
-                def _():
-                    for event in todo:
-                        act_on(event, role)
-
-    for event in events:
-        if event[1] == "all":
-            flush()
-            act_on(event, "all")
-        else:
-            pending[event[1]].append(event)
-    flush()
+    @pl.when(cz < co - 1)
+    def _():
+        pl.semaphore_wait(sem_up, (co - 1 - cz) * ci)
+
+
+    @pl.when(central)
+    def _():
+        seen = []
+        for event in CENTRAL:
+            act_on(event, "cen", seen)
+
+    @pl.when(jnp.logical_not(central))
+    def _():
+        seen = []
+        for event in RIM:
+            act_on(event, "rim", seen)
 
     block = gathered(*final)
     last = ghs[block]
@@ -469,16 +446,22 @@
             lax.rem(rx + d, ro) * ri + rc,
         )
 
-    targets = list(range(1, ro)) + [0]
-    for d in targets:
+    def to_siblings(d):
         to = lax.rem(rx + d, ro)
         for e in range(1, ri):
             rs_y[d * (ri - 1) + e - 1] = finished(to, lax.rem(rc + e, ri)).astype(BF16)
             for p in range(parts):
                 sibling(d, e, p).start()
-    for d in targets:
+
+    def kept(d):
         at = rows(lax.rem(rx + d, ro) * ri + rc)
         acc[at, :] = finished(lax.rem(rx + d, ro), rc)
+
+    for d in range(1, ro):
+        to_siblings(d)
+    for d in range(1, ro):
+        kept(d)
+    to_siblings(0)
 
     def chip_sum(d, p):
         at = pl.ds(pl.multiple_of((lax.rem(rx + d, ro) * ri + rc) * own + p * piece, piece), piece)
@@ -493,6 +476,7 @@
                 pieces(ri - 1, sem_ry.at[(d - 1) * parts + p])
             rs_z[d - 1, cut(p)] = chip_sum(d, p).astype(BF16)
             across(d, p).start()
+    kept(0)
     weight_step(3)
     if ri > 1:
         at = rr_y.at[pl.ds(0, ri - 1)]
@@ -542,7 +526,7 @@
     ro, ri = split_axis(nrow, 2)
     co = 4
     ci = ncol // co
-    parts = 4
+    parts = PARTS
     dims = (nrow, ncol, ro, ri, co, ci, parts)
 
     def body(features, weight, grad_out, adj_values, block_pos, block_count):
@@ -586,6 +570,7 @@
             block(ncol - 1, rows2),
             pltpu.VMEM((ncol, nrow, rows2, width), BF16),
             dma((5,)),
+            pltpu.SemaphoreType.REGULAR,
             dma((1,)),
             dma((max(2 * (ro - 1), 1),)),
             dma((1,)),

time: 47.8 us -> 47.3 us (0.990)
  Pallas kernels: 46.4 us -> 45.8 us
    pallas_call x1, Pallas kernels: 45.6 us -> 45 us  [body(): pl.pallas_call(functools.partial(kernel, dims), out_shape=shapes, in_spec...]
where the time goes in v2:
time: 47.3 us; the launch traced here: 47.1 us
  Pallas kernels  45.8 us (97%)
  between operations  1.29 us (3%)
    pallas_call x1, Pallas kernels, body(): pl.pallas_call(functools.partial(kernel, dims), out_shape=shapes, in_spec...  45 us

profile of v2, /device:TPU:0, one launch (start us, length us, event | category | flops | bytes accessed | tf_op | source)
XLA Modules:
  0.0 47.1 jit_solution(12812384379496142570)
XLA Ops:
  1.3 45.0 %shard_map.85 = (bf16[256,256]{1,0:T(8,128)(2,1)S(1)}, bf16[256,256]{1,0:T(8,128)(2,1)S(1)}, f32[256,256]{1,0:T(8,128)S(1)}) custom-call(s32[1,1]{1,0:T(1,128)S(6)} %copy.9.count_ref, s32[1,96]{1,0:T(1,128)} %pos_ref.1, bf16[256,256]{1,0:T(8,128)(2,1)} %feat_ref.1, bf16[256,256]{1,0:T(8,128)(2,1)} %weight_ref.1, bf16[256,256]{1,0:T(8,128)(2,1)} %gout_ref.1, ...), custom_call_target="tpu_custom_call" | custom-call | tf_op jit(solution)/shard_map/pallas_call | solution.py:597
  46.3 0.8 %shard_map.86 = (bf16[256,256]{1,0:T(8,128)(2,1)}, bf16[256,256]{1,0:T(8,128)(2,1)}, f32[256,256]{1,0:T(8,128)}) custom-call(bf16[256,256]{1,0:T(8,128)(2,1)S(1)} %get-tuple-element.6.a_in, bf16[256,256]{1,0:T(8,128)(2,1)S(1)} %get-tuple-element.7.b_in, f32[256,256]{1,0:T(8,128)S(1)} %get-tuple-element.8.c_in), custom_call_target="tpu_custom_call" | custom-call | tf_op jit(solution)/shard_map/pallas_call | solution.py:615

commit v3 on v2

--- a/solution.py
+++ b/solution.py
@@ -11,30 +11,41 @@
 F32 = jnp.float32
 BF16 = jnp.bfloat16
 OWN, MATE, NEAR, FAR = 0, 1, 2, 3
-PARTS = 4
+PARTS = 8
+TAIL = 4
 ORDER = (
-    (0, 2), (0, 3), (2, 3), (1, 3), (1, 2), (0, 1), (3, 3), (3, 2),
-    (2, 2), (3, 1), (1, 1), (2, 1), (0, 0), (1, 0), (2, 0), (3, 0),
+    (0, 2), (0, 3), (0, 1), (1, 3), (3, 2), (4, 3), (5, 3), (3, 3),
+    (7, 3), (6, 2), (1, 2), (4, 2), (3, 1), (2, 2), (4, 1), (2, 3),
+    (7, 2), (6, 3), (0, 0), (3, 0), (5, 2), (1, 1), (6, 1), (7, 1),
+    (5, 1), (2, 1), (2, 0), (1, 0), (4, 0), (7, 0), (6, 0), (5, 0),
 )
 RIM = (
-    ("P", 2, 0), ("P", 3, 0), ("P", 1, 0), ("M", 0, 2), ("P", 0, 0), ("M", 0, 3),
-    ("M", 2, 3), ("M", 1, 3), ("M", 1, 2), ("M", 0, 1), ("M", 3, 3), ("M", 3, 2),
-    ("M", 2, 2), ("M", 3, 1), ("M", 1, 1), ("M", 2, 1), ("E", 0, 0), ("E", 1, 0),
-    ("E", 2, 0), ("E", 3, 0), ("W", 0, 0), ("B", 0, 0), ("O", 0, 1), ("O", 1, 1),
-    ("O", 3, 1), ("O", 0, 2), ("W", 1, 0), ("O", 2, 1), ("B", 1, 0), ("O", 0, 3),
-    ("O", 1, 2), ("O", 3, 2), ("O", 1, 3), ("O", 2, 2), ("B", 2, 0), ("O", 2, 3),
-    ("O", 3, 3), ("B", 3, 0), ("B", 0, 1), ("B", 1, 1), ("W", 2, 0), ("B", 2, 1),
-    ("B", 3, 1),
+    ("P", 2, 0), ("P", 3, 0), ("M", 0, 2), ("P", 1, 0), ("M", 0, 3), ("P", 0, 0),
+    ("M", 0, 1), ("M", 1, 3), ("M", 3, 2), ("M", 4, 3), ("M", 5, 3), ("M", 3, 3),
+    ("M", 7, 3), ("M", 6, 2), ("M", 1, 2), ("M", 4, 2), ("M", 3, 1), ("M", 2, 2),
+    ("M", 4, 1), ("M", 2, 3), ("M", 7, 2), ("M", 6, 3), ("E", 0, 0), ("M", 5, 2),
+    ("M", 1, 1), ("M", 6, 1), ("M", 7, 1), ("E", 3, 0), ("M", 5, 1), ("M", 2, 1),
+    ("O", 0, 1), ("O", 3, 1), ("E", 1, 0), ("E", 4, 0), ("E", 7, 0), ("E", 5, 0),
+    ("O", 0, 2), ("E", 2, 0), ("O", 3, 2), ("E", 6, 0), ("W", 0, 0), ("O", 4, 1),
+    ("B", 0, 0), ("O", 1, 1), ("O", 0, 3), ("O", 6, 1), ("O", 7, 1), ("O", 3, 3),
+    ("O", 2, 1), ("O", 5, 1), ("B", 1, 0), ("O", 4, 2), ("W", 1, 0), ("O", 1, 2),
+    ("O", 6, 2), ("O", 1, 3), ("O", 7, 2), ("O", 4, 3), ("O", 2, 2), ("O", 7, 3),
+    ("O", 5, 2), ("B", 2, 0), ("O", 5, 3), ("O", 2, 3), ("O", 6, 3), ("B", 3, 0),
+    ("B", 0, 1), ("B", 1, 1), ("W", 2, 0), ("B", 2, 1), ("B", 3, 1),
 )
 CENTRAL = (
-    ("P", 2, 0), ("P", 3, 0), ("P", 1, 0), ("P", 0, 0), ("J", 0, 2), ("M", 0, 1),
-    ("J", 0, 3), ("J", 2, 3), ("J", 1, 3), ("J", 1, 2), ("M", 3, 1), ("M", 1, 1),
-    ("J", 3, 3), ("M", 2, 1), ("J", 3, 2), ("E", 0, 0), ("J", 2, 2), ("E", 1, 0),
-    ("E", 3, 0), ("O", 0, 2), ("O", 0, 1), ("E", 2, 0), ("W", 0, 0), ("B", 0, 0),
-    ("O", 0, 3), ("O", 1, 2), ("O", 1, 1), ("O", 3, 2), ("O", 1, 3), ("O", 2, 1),
-    ("O", 2, 2), ("W", 1, 0), ("B", 2, 0), ("O", 2, 3), ("O", 3, 1), ("B", 1, 0),
-    ("O", 3, 3), ("B", 3, 0), ("B", 0, 1), ("B", 2, 1), ("W", 2, 0), ("B", 1, 1),
-    ("B", 3, 1),
+    ("P", 2, 0), ("P", 3, 0), ("P", 1, 0), ("P", 0, 0), ("M", 0, 1), ("J", 0, 2),
+    ("J", 0, 3), ("J", 1, 3), ("J", 3, 2), ("M", 3, 1), ("J", 4, 3), ("J", 5, 3),
+    ("M", 4, 1), ("J", 3, 3), ("J", 7, 3), ("J", 6, 2), ("J", 1, 2), ("E", 0, 0),
+    ("J", 4, 2), ("E", 3, 0), ("J", 2, 2), ("M", 1, 1), ("M", 6, 1), ("J", 2, 3),
+    ("M", 7, 1), ("J", 7, 2), ("M", 5, 1), ("J", 6, 3), ("M", 2, 1), ("O", 0, 2),
+    ("O", 0, 1), ("J", 5, 2), ("O", 3, 2), ("E", 4, 0), ("E", 1, 0), ("O", 0, 3),
+    ("E", 6, 0), ("E", 7, 0), ("O", 3, 1), ("O", 3, 3), ("E", 2, 0), ("E", 5, 0),
+    ("W", 0, 0), ("O", 4, 2), ("B", 0, 0), ("O", 1, 1), ("O", 1, 2), ("O", 6, 2),
+    ("O", 4, 1), ("O", 1, 3), ("O", 7, 2), ("O", 7, 1), ("O", 4, 3), ("O", 2, 2),
+    ("O", 5, 1), ("O", 7, 3), ("O", 5, 2), ("B", 2, 0), ("O", 2, 1), ("W", 1, 0),
+    ("O", 5, 3), ("O", 2, 3), ("O", 6, 1), ("B", 1, 0), ("O", 6, 3), ("B", 3, 0),
+    ("B", 0, 1), ("B", 2, 1), ("W", 2, 0), ("B", 1, 1), ("B", 3, 1),
 )
 
 
@@ -425,23 +436,32 @@
             dense_t[at, rows(block)], last, preferred_element_type=F32
         )
 
+    chunk = own // TAIL
+
+    def tail_cut(p):
+        return pl.ds(p * chunk, chunk)
+
+    def tail_pieces(n, sem):
+        at = rr_y.at[pl.ds(0, n), tail_cut(0)]
+        remote(at, at, sem_sent.at[0], sem, "row", 0).wait_recv()
+
     def sibling(d, e, p):
         at = d * (ri - 1) + e - 1
         return remote(
-            rs_y.at[at, cut(p)],
-            rr_y.at[at, cut(p)],
+            rs_y.at[at, tail_cut(p)],
+            rr_y.at[at, tail_cut(p)],
             sem_sent.at[0],
-            sem_ry.at[(d - 1) * parts + p] if d else sem_r0.at[0],
+            sem_ry.at[(d - 1) * TAIL + p] if d else sem_r0.at[0],
             "row",
             rx * ri + lax.rem(rc + e, ri),
         )
 
     def across(d, p):
         return remote(
-            rs_z.at[d - 1, cut(p)],
-            rr_z.at[d - 1, cut(p)],
+            rs_z.at[d - 1, tail_cut(p)],
+            rr_z.at[d - 1, tail_cut(p)],
             sem_sent.at[0],
-            sem_rz.at[(d - 1) * parts + p],
+            sem_rz.at[(d - 1) * TAIL + p],
             "row",
             lax.rem(rx + d, ro) * ri + rc,
         )
@@ -450,7 +470,7 @@
         to = lax.rem(rx + d, ro)
         for e in range(1, ri):
             rs_y[d * (ri - 1) + e - 1] = finished(to, lax.rem(rc + e, ri)).astype(BF16)
-            for p in range(parts):
+            for p in range(TAIL):
                 sibling(d, e, p).start()
 
     def kept(d):
@@ -464,29 +484,29 @@
     to_siblings(0)
 
     def chip_sum(d, p):
-        at = pl.ds(pl.multiple_of((lax.rem(rx + d, ro) * ri + rc) * own + p * piece, piece), piece)
+        at = pl.ds(pl.multiple_of((lax.rem(rx + d, ro) * ri + rc) * own + p * chunk, chunk), chunk)
         value = acc[at, :]
         for e in range(1, ri):
-            value = value + rr_y[d * (ri - 1) + e - 1, cut(p)].astype(F32)
+            value = value + rr_y[d * (ri - 1) + e - 1, tail_cut(p)].astype(F32)
         return value
 
-    for p in range(parts):
+    for p in range(TAIL):
         for d in range(1, ro):
             if ri > 1:
-                pieces(ri - 1, sem_ry.at[(d - 1) * parts + p])
-            rs_z[d - 1, cut(p)] = chip_sum(d, p).astype(BF16)
+                tail_pieces(ri - 1, sem_ry.at[(d - 1) * TAIL + p])
+            rs_z[d - 1, tail_cut(p)] = chip_sum(d, p).astype(BF16)
             across(d, p).start()
     kept(0)
     weight_step(3)
     if ri > 1:
         at = rr_y.at[pl.ds(0, ri - 1)]
         remote(at, at, sem_sent.at[0], sem_r0.at[0], "row", 0).wait_recv()
-    for p in range(parts):
+    for p in range(TAIL):
         value = chip_sum(0, p)
         for d in range(1, ro):
             across(d, p).wait_recv()
-            value = value + rr_z[d - 1, cut(p)].astype(F32)
-        gin_ref[cut(p), :] = lax.dot_general(
+            value = value + rr_z[d - 1, tail_cut(p)].astype(F32)
+        gin_ref[tail_cut(p), :] = lax.dot_general(
             value.astype(BF16), pair[0], (((1,), (1,)), ((), ())), preferred_element_type=F32
         ).astype(BF16)
     weight_step(4)
@@ -577,9 +597,9 @@
             dma((parts * 4,)),
             dma((parts * 3,)),
             dma((max(co * (ci - 1), 1),)),
-            dma((max(parts * (ro - 1), 1),)),
+            dma((max(TAIL * (ro - 1), 1),)),
             dma((1,)),
-            dma((max(parts * (ro - 1), 1),)),
+            dma((max(TAIL * (ro - 1), 1),)),
             dma((2, 4)),
         ]
         vmem = pl.BlockSpec(memory_space=pltpu.VMEM)

time: 47.3 us -> 45.9 us (0.970)
  Pallas kernels: 45.8 us -> 44.4 us
    pallas_call x1, Pallas kernels: 45 us -> 43.6 us  [body(): pl.pallas_call(functools.partial(kernel, dims), out_shape=shapes, in_spec...]
where the time goes in v3:
time: 45.9 us; the launch traced here: 45.7 us
  Pallas kernels  44.4 us (97%)
  between operations  1.29 us (3%)
    pallas_call x1, Pallas kernels, body(): pl.pallas_call(functools.partial(kernel, dims), out_shape=shapes, in_spec...  43.6 us

profile of v3, /device:TPU:0, one launch (start us, length us, event | category | flops | bytes accessed | tf_op | source)
XLA Modules:
  0.0 45.7 jit_solution(16206950493384333015)
XLA Ops:
  1.3 43.6 %shard_map.85 = (bf16[256,256]{1,0:T(8,128)(2,1)S(1)}, bf16[256,256]{1,0:T(8,128)(2,1)S(1)}, f32[256,256]{1,0:T(8,128)S(1)}) custom-call(s32[1,1]{1,0:T(1,128)S(6)} %copy.9.count_ref, s32[1,96]{1,0:T(1,128)} %pos_ref.1, bf16[256,256]{1,0:T(8,128)(2,1)} %feat_ref.1, bf16[256,256]{1,0:T(8,128)(2,1)} %weight_ref.1, bf16[256,256]{1,0:T(8,128)(2,1)} %gout_ref.1, ...), custom_call_target="tpu_custom_call" | custom-call | tf_op jit(solution)/shard_map/pallas_call | solution.py:617
  44.9 0.8 %shard_map.86 = (bf16[256,256]{1,0:T(8,128)(2,1)}, bf16[256,256]{1,0:T(8,128)(2,1)}, f32[256,256]{1,0:T(8,128)}) custom-call(bf16[256,256]{1,0:T(8,128)(2,1)S(1)} %get-tuple-element.6.a_in, bf16[256,256]{1,0:T(8,128)(2,1)S(1)} %get-tuple-element.7.b_in, f32[256,256]{1,0:T(8,128)S(1)} %get-tuple-element.8.c_in), custom_call_target="tpu_custom_call" | custom-call | tf_op jit(solution)/shard_map/pallas_call | solution.py:635
